TPU v7x, 32 devices: a whole 2x2x4 slice. The times are simulated.
32 devices in a mesh: rows: 8 (over z, core), cols: 4 (over y, x).
Axes of the slice: x: 2, y: 2, z: 4, core: 2. Of those that a mesh axis runs over, the one named last changes fastest.
Arguments:
- left_factor: float32 [2048, 2048], P('rows', 'cols'), may hold values from -0.125 to 0.125
- left_cot: float32 [2048, 2048], P('rows', 'cols'), may hold values from -6 to 6
- panel_factor: float32 [2, 256, 2048], P(None, 'cols', 'rows'), may hold values from -0.125 to 0.125
- panel_cot: float32 [2, 256, 2048], P(None, 'cols', 'rows'), may hold values from -6 to 6
- rows_factor: float32 [2, 256, 2048], P(None, 'rows', 'cols'), may hold values from -0.375 to 0.375
- rows_cot: float32 [2, 256, 2048], P(None, 'rows', 'cols'), may hold values from -6 to 6
- cross_factor: float32 [256, 256], P('cols', 'rows'), may hold values from -0.375 to 0.375
- cross_cot: float32 [256, 256], P('cols', 'rows'), may hold values from -6 to 6
- diag_factor: float32 [2, 256, 256], P(None, 'rows'), as said below
- diag_cot: float32 [2, 256, 256], P(None, 'rows'), may hold values from -6 to 6
Outputs:
- left_bar: float32 [2048, 2048], P('rows', 'cols')
- rows_bar: float32 [2, 256, 2048], P(None, 'rows', 'cols')
- panel_bar: float32 [2, 256, 2048], P(None, 'cols', 'rows')
- cross_bar: float32 [256, 256], P('cols', 'rows')
- diag_bar: float32 [2, 256, 256], P(None, 'rows')
Inputs may be any that keep to these rules, and one draw needn't show every extreme that they name: `diag_factor`: each of the two blocks is lower triangular, with diagonal entries from 0.75 to 1.5; the entries below the diagonal are drawn independently with mean zero and spread at most 0.35 / sqrt(256), each of magnitude at most 1.4 / sqrt(256).
All inputs are finite; a program needn't handle non-finite values.
Results may differ from a plain program's by a relative error of at most 0.00016.
Values sent between devices are 32-bit elements; how exact they have to be, the bound alone decides.
No kernel may reach another device: no remote copies, remote signals or barrier semaphores. Data moves between devices by JAX's collectives and lax.ppermute only.
A program may use at most 64 MiB of HBM per device.

v0:
```python
import jax
import jax.numpy as jnp
from jax import lax
from jax.sharding import PartitionSpec as P

highest = lax.Precision.HIGHEST


def product(former, latter):
    return jnp.dot(former, latter, precision=highest, preferred_element_type=jnp.float32)


def halved_lower(matrix):
    return jnp.tril(matrix) - 0.5 * jnp.diag(jnp.diag(matrix))


def solve_upper(factor, values):
    return lax.linalg.triangular_solve(factor, values, left_side=True, lower=True, transpose_a=True)


def reverse_block(factor, pending):
    shaped = halved_lower(product(factor.T, pending))
    middle = solve_upper(factor, shaped)
    transposed = solve_upper(factor, middle.T)
    return transposed + transposed.T


def panel_solve(factor_cols, cot_cols, diag_whole, pending_cot):
    cot_whole = lax.all_gather(cot_cols, "cols", axis=0, tiled=True)
    solved = solve_upper(diag_whole, cot_whole)
    narrow = lax.psum(product(solved, factor_cols.T), "rows")
    partial_value = lax.all_gather(narrow, "cols", axis=1, tiled=True)
    return (solved, pending_cot - jnp.tril(partial_value))


def on_device(
    left_factor,
    left_cot,
    panel_factor,
    panel_cot,
    rows_factor,
    rows_cot,
    cross_factor,
    cross_cot,
    diag_factor,
    diag_cot,
):
    row_share = rows_factor.shape[1]
    col_share = panel_factor.shape[1]
    row_start = lax.axis_index("rows") * row_share
    col_start = lax.axis_index("cols") * col_share
    diag_whole, diag_cot_whole = (
        lax.all_gather(diag_factor, "rows", axis=1, tiled=True),
        lax.all_gather(diag_cot, "rows", axis=1, tiled=True),
    )
    upper_whole, cross_whole = (
        lax.all_gather(rows_factor[1], "rows", axis=0, tiled=True),
        lax.all_gather(cross_factor, "rows", axis=1, tiled=True),
    )
    solved_two, pending_two = panel_solve(
        panel_factor[1], panel_cot[1], diag_whole[1], diag_cot_whole[1]
    )
    left_next = left_cot - product(solved_two.T, upper_whole)
    first_cot = panel_cot[0] - product(cross_whole, solved_two)
    sym_two = reverse_block(diag_whole[1], pending_two)
    sym_rows = lax.dynamic_slice_in_dim(sym_two, row_start, row_share, 0)
    upper_local = product(solved_two, left_factor)
    cross_local = product(panel_factor[0], solved_two.T)
    upper_term, cross_term = (
        lax.psum_scatter(upper_local, "rows", scatter_dimension=0, tiled=True),
        lax.psum_scatter(cross_local, "rows", scatter_dimension=1, tiled=True),
    )
    upper_rows = rows_cot[1] - upper_term - product(sym_rows, upper_whole)
    cross_next = (
        cross_cot
        - cross_term
        - product(cross_whole, lax.dynamic_slice_in_dim(sym_two, row_start, row_share, 1))
    )
    lower_whole = lax.all_gather(rows_factor[0], "rows", axis=0, tiled=True)
    factor_cols = jnp.concatenate([cross_factor, panel_factor[0]], axis=1)
    cot_cols = jnp.concatenate([cross_next, first_cot], axis=1)
    solved_one, pending_one = panel_solve(factor_cols, cot_cols, diag_whole[0], diag_cot_whole[0])
    cross_part = solved_one[:, :row_share]
    lower_part = solved_one[:, row_share:]
    upper_rows = upper_rows - product(cross_part.T, lower_whole)
    left_next = left_next - product(lower_part.T, lower_whole)
    sym_one = reverse_block(diag_whole[0], pending_one)
    lower_local = product(cross_part, rows_factor[1]) + product(lower_part, left_factor)
    lower_term = lax.psum_scatter(lower_local, "rows", scatter_dimension=0, tiled=True)
    lower_rows = (
        rows_cot[0]
        - lower_term
        - product(lax.dynamic_slice_in_dim(sym_one, row_start, row_share, 0), lower_whole)
    )

    def own_cols(matrix):
        return lax.dynamic_slice_in_dim(matrix, col_start, col_share, 0)

    panel_out = jnp.stack([own_cols(lower_part), own_cols(solved_two)])
    cross_out = own_cols(cross_part)
    diag_out = jnp.stack(
        [
            lax.dynamic_slice_in_dim(halved_lower(sym_one), row_start, row_share, 0),
            lax.dynamic_slice_in_dim(halved_lower(sym_two), row_start, row_share, 0),
        ]
    )
    return (left_next, jnp.stack([lower_rows, upper_rows]), panel_out, cross_out, diag_out)


def solution(mesh):
    placed = (
        P("rows", "cols"),
        P("rows", "cols"),
        P(None, "cols", "rows"),
        P(None, "cols", "rows"),
        P(None, "rows", "cols"),
        P(None, "rows", "cols"),
        P("cols", "rows"),
        P("cols", "rows"),
        P(None, "rows", None),
        P(None, "rows", None),
    )
    return jax.shard_map(
        on_device,
        mesh=mesh,
        in_specs=placed,
        out_specs=(
            P("rows", "cols"),
            P(None, "rows", "cols"),
            P(None, "cols", "rows"),
            P("cols", "rows"),
            P(None, "rows", None),
        ),
        check_vma=False,
    )
```

profile of v0, /device:TPU:0, one launch (start us, length us, event | category | flops | bytes accessed | tf_op | source)
XLA Modules:
  0.0 286.8 jit_solution(2854972493506229909)
XLA Ops:
  8.2 16.5 %all_gather.27 = f32[2,256,256]{2,0,1:T(2,128)S(1)} all-gather(f32[2,32,256]{2,0,1:T(2,128)S(1)} %copy.44), channel_id=1, replica_groups=mesh['rows'=8,'cols'=4] {'rows'}, dimensions={1}, use_global_device_ids=true | all-gather | bytes 589824 | tf_op jit(solution)/shard_map/all_gather | solution.py:53
  25.2 4.0 %while.12 = (s32[]{:T(128)}, f32[256,256]{1,0:T(8,128)S(1)}, s32[2,2]{1,0:T(2,128)S(1)}, f32[2,128,128]{2,1,0:T(8,128)S(1)}, s32[]{:T(128)}) while((s32[]{:T(128)}, f32[256,256]{1,0:T(8,128)S(1)}, s32[2,2]{1,0:T(2,128)S(1)}, f32[2,128,128]{2,1,0:T(8,128)S(1)}, s32[]{:T(128)}) %tuple.71), condition=%wide.while_cond, body=%wide.while_body.sunk | while | flops 2 | bytes 131181 | solution.py:18
  29.2 19.7 %custom-call.19 = f32[2,128,128]{1,2,0:T(8,128)S(1)} custom-call(f32[2,128,128]{2,1,0:T(8,128)S(1)} %get-tuple-element.46), custom_call_target="InvertDiagBlocksLowerTriangular" | custom-call | tf_op jit(solution)/shard_map/triangular_solve/custom-call.1 | solution.py:18
  49.7 9.0 %all-gather = f32[1,256,256]{2,1,0:T(8,128)S(1)} all-gather(f32[1,64,256]{2,1,0:T(8,128)S(1)} %slice-done), channel_id=2, replica_groups=mesh['rows'=8,'cols'=4] {'cols'}, dimensions={1}, use_global_device_ids=true | all-gather | bytes 327680 | tf_op jit(solution)/shard_map/all_gather | solution.py:29
  63.2 14.1 %all_gather.32 = f32[64,256]{0,1:T(8,128)S(1)} all-gather(f32[64,32]{0,1:T(8,128)S(1)} %copy-done.12), channel_id=1, replica_groups=mesh['rows'=8,'cols'=4] {'rows'}, dimensions={1}, use_global_device_ids=true | all-gather | bytes 73728 | tf_op jit(solution)/shard_map/all_gather | solution.py:58
  77.5 14.9 %all_gather.30 = f32[2,256,256]{2,0,1:T(2,128)S(1)} all-gather(f32[2,32,256]{2,0,1:T(2,128)S(1)} %copy.48), channel_id=1, replica_groups=mesh['rows'=8,'cols'=4] {'rows'}, dimensions={1}, use_global_device_ids=true | all-gather | bytes 589824 | tf_op jit(solution)/shard_map/all_gather | solution.py:54
  94.2 4.2 %while.11 = (s32[]{:T(128)}, f32[256,256]{0,1:T(8,128)S(1)}, s32[2,2]{1,0:T(2,128)S(1)}, f32[2,128,128]{2,1,0:T(8,128)S(1)}, s32[]{:T(128)}) while((s32[]{:T(128)}, f32[256,256]{0,1:T(8,128)S(1)}, s32[2,2]{1,0:T(2,128)S(1)}, f32[2,128,128]{2,1,0:T(8,128)S(1)}, s32[]{:T(128)}) %tuple.87), condition=%wide.while_cond.1, body=%wide.while_body.1.sunk | while | flops 2 | bytes 393321 | solution.py:18
  98.5 19.7 %custom-call.6 = f32[2,128,128]{1,2,0:T(8,128)S(1)} custom-call(f32[2,128,128]{2,1,0:T(8,128)S(1)} %get-tuple-element.21), custom_call_target="InvertDiagBlocksLowerTriangular" | custom-call | tf_op jit(solution)/shard_map/triangular_solve | solution.py:18
  118.2 9.1 %all_gather.31 = f32[256,256]{0,1:T(8,128)S(1)} all-gather(f32[256,64]{0,1:T(8,128)} %all-reduce.3.cloned.1.call-done), channel_id=1, replica_groups=mesh['rows'=8,'cols'=4] {'cols'}, dimensions={1}, use_global_device_ids=true | all-gather | bytes 327680 | tf_op jit(solution)/shard_map/all_gather | solution.py:32
  127.7 2.4 gather_fusion
  132.3 16.6 %reduce-scatter.10.cloned.1.call-done = f32[32,64]{1,0:T(8,128)} async-done(((f32[256,64]{1,0:T(8,128)}), f32[32,64]{1,0:T(8,128)}) %reduce-scatter.10.cloned.1.call-update) | async-done | bytes 8208
  150.1 9.5 %all_gather.33 = f32[256,288]{1,0:T(8,128)S(1)} all-gather(f32[64,288]{1,0:T(8,128)S(1)} %pad_maximum_fusion.7), channel_id=1, replica_groups=mesh['rows'=8,'cols'=4] {'cols'}, dimensions={0}, use_global_device_ids=true | all-gather | bytes 368640 | tf_op jit(solution)/shard_map/all_gather | solution.py:29
  165.1 15.0 %all-gather.2 = f32[1,256,512]{2,1,0:T(8,128)S(1)} all-gather(f32[1,32,512]{2,1,0:T(8,128)S(1)} %get-tuple-element.137), channel_id=4, replica_groups=mesh['rows'=8,'cols'=4] {'rows'}, dimensions={1}, use_global_device_ids=true | all-gather | bytes 589824 | tf_op jit(solution)/shard_map/all_gather | solution.py:79
  180.0 15.0 %all-gather.1 = f32[1,256,512]{2,1,0:T(8,128)S(1)} all-gather(f32[1,32,512]{2,1,0:T(8,128)S(1)} %get-tuple-element.138), channel_id=3, replica_groups=mesh['rows'=8,'cols'=4] {'rows'}, dimensions={1}, use_global_device_ids=true | all-gather | bytes 589824 | tf_op jit(solution)/shard_map/all_gather | solution.py:57
  195.7 1.7 convolution_subtract_fusion.1
  197.4 2.4 gather_fusion.3
  202.1 1.4 convolution_add_fusion
  203.5 1.4 convolution_subtract_fusion
  206.4 7.9 %all-reduce.5.cloned.1.call-done = f32[256,64]{0,1:T(8,128)} async-done(((f32[256,64]{0,1:T(8,128)}), f32[256,64]{0,1:T(8,128)}) %all-reduce.5.cloned.1.call-update) | async-done | bytes 65552 | tf_op jit(solution)/shard_map/psum | solution.py:31
  214.3 9.6 %all_gather.35 = f32[256,256]{0,1:T(8,128)S(1)} all-gather(f32[256,64]{0,1:T(8,128)} %all-reduce.5.cloned.1.call-done), channel_id=1, replica_groups=mesh['rows'=8,'cols'=4] {'cols'}, dimensions={1}, use_global_device_ids=true | all-gather | bytes 327680 | tf_op jit(solution)/shard_map/all_gather | solution.py:32
  224.4 2.4 gather_fusion.1
  229.8 2.4 gather_fusion.2
  233.3 13.5 %reduce-scatter.8.cloned.1.call-done = f32[32,512]{1,0:T(8,128)} async-done(((f32[256,512]{1,0:T(8,128)}), f32[32,512]{1,0:T(8,128)}) %reduce-scatter.8.cloned.1.call-update) | async-done | bytes 65552 | tf_op jit(solution)/shard_map/reduce_scatter | solution.py:70
  248.1 30.2 %reduce-scatter.6.cloned.1.call-done = f32[32,512]{1,0:T(8,128)} async-done(((f32[256,512]{1,0:T(8,128)}), f32[32,512]{1,0:T(8,128)}) %reduce-scatter.6.cloned.1.call-update) | async-done | bytes 65552 | tf_op jit(solution)/shard_map/reduce_scatter | solution.py:89
  (134 shorter events, 38.0 us)
Async XLA Ops:
  7.2 154.8 %copy-start = (f32[256,512]{1,0:T(8,128)S(1)}, f32[256,512]{1,0:T(8,128)}, u32[]{:S(2)}) copy-start(f32[256,512]{1,0:T(8,128)} %param.12) | copy-start | bytes 1572868
  7.2 111.0 %all-reduce.3.cloned.1.call-start = ((), (), s32[]{:S(2)}) async-start(), calls=%async_computation.3 | async-start | bytes 131072 | tf_op jit(solution)/shard_map/psum | solution.py:31
  48.9 0.8 slice-start
  59.3 0.9 copy-start.6
  61.2 87.7 %reduce-scatter.10.cloned.1.call-start = ((), (), s32[]{:S(2)}) async-start(), calls=%async_computation.7 | async-start | bytes 147456
  62.5 151.9 %all-reduce.5.cloned.1.call-start = ((), (), s32[]{:S(2)}) async-start(), calls=%async_computation.5 | async-start | bytes 131072 | tf_op jit(solution)/shard_map/psum | solution.py:31
  62.5 0.7 copy-start.12
  63.2 14.2 %copy-start.13 = (f32[2,32,256]{2,1,0:T(8,128)S(1)}, f32[2,32,256]{2,1,0:T(8,128)}, u32[]{:S(2)}) copy-start(f32[2,32,256]{2,1,0:T(8,128)} %param.21) | copy-start | bytes 196612
  92.7 0.9 copy-start.7
  118.2 42.2 %copy-start.1 = (f32[2,128,128]{1,2,0:T(8,128)}, f32[2,128,128]{1,2,0:T(8,128)S(1)}, u32[]{:S(2)}) copy-start(f32[2,128,128]{1,2,0:T(8,128)S(1)} %custom-call.6) | copy-start | bytes 393220
  132.3 16.7 %copy-start.14 = (f32[64,32]{0,1:T(8,128)S(1)}, f32[64,32]{0,1:T(8,128)}, u32[]{:S(2)}) copy-start(f32[64,32]{0,1:T(8,128)} %param.19) | copy-start | bytes 24580
  161.9 84.9 %reduce-scatter.8.cloned.1.call-start = ((), (), s32[]{:S(2)}) async-start(), calls=%async_computation.6 | async-start | bytes 589824 | tf_op jit(solution)/shard_map/reduce_scatter | solution.py:70
  163.4 114.9 %reduce-scatter.6.cloned.1.call-start = ((), (), s32[]{:S(2)}) async-start(), calls=%async_computation.4 | async-start | bytes 589824 | tf_op jit(solution)/shard_map/reduce_scatter | solution.py:89
  164.2 0.9 copy-start.4
  201.1 0.9 copy-start.5
  204.9 0.8 copy-start.8
  205.8 18.2 %copy-start.3 = (f32[1,256,256]{1,2,0:T(8,128)S(1)}, f32[1,256,256]{1,2,0:T(8,128)}, u32[]{:S(2)}) copy-start(f32[1,256,256]{1,2,0:T(8,128)} %copy.76) | copy-start | bytes 786436
  226.7 0.9 copy-start.2
  229.8 2.5 copy-start.9
  229.8 2.5 copy-start.10
  232.6 14.2 %copy-start.11 = (f32[2,32,512]{2,1,0:T(8,128)S(1)}, f32[2,32,512]{2,1,0:T(8,128)}, u32[]{:S(2)}) copy-start(f32[2,32,512]{2,1,0:T(8,128)} %param.17) | copy-start | bytes 393220
Sparse Core Ops, SparseCore 0:
  61.4 55.0 all-reduce.2
  119.3 29.6 reduce-scatter.9
  162.0 52.2 all-reduce.4
  216.4 30.2 reduce-scatter.7
  248.9 29.3 reduce-scatter.5
where the time goes:
time: 288 us; the launch traced here: 287 us
  blocking collectives  113 us (39%)
  waiting for transfers between devices  68.3 us (24%)
  other arithmetic  43.3 us (15%)
  local copies, waits for them, and re-layouts  27.9 us (10%)
  matrix products  19.9 us (7%)
  between operations  14.4 us (5%)
    another operation x9, other arithmetic, solve_upper(): lax.linalg.triangular_solve(factor, values, left_side=True, lower=True, t...  39.5 us
    reduce_scatter x1, waiting for transfers between devices, on_device(): lax.psum_scatter(lower_local, 'rows', scatter_dimension=0, tiled=True)  30.2 us
    all_gather x2, blocking collectives, panel_solve(): partial_value = lax.all_gather(narrow, 'cols', axis=1, tiled=True)  18.8 us
    all_gather x2, blocking collectives, panel_solve(): cot_whole = lax.all_gather(cot_cols, 'cols', axis=0, tiled=True)  18.5 us
    unnamed x6, waiting for transfers between devices  16.7 us
    all_gather x1, blocking collectives, on_device(): lax.all_gather(diag_factor, 'rows', axis=1, tiled=True)  16.5 us
    all_gather x1, blocking collectives, on_device(): lax.all_gather(rows_factor[1], 'rows', axis=0, tiled=True)  15 us
    all_gather x1, blocking collectives, on_device(): lower_whole = lax.all_gather(rows_factor[0], 'rows', axis=0, tiled=True)  15 us
  transfers between devices with their start and end apart: 5, of which 4 were waited for; matrix products, arithmetic and copies ran while one was open for 19% of the time, Pallas kernels for 0%

commit v1 on v0

--- a/solution.py
+++ b/solution.py
@@ -4,6 +4,23 @@
 from jax.sharding import PartitionSpec as P
 
 highest = lax.Precision.HIGHEST
+
+
+def joined_along(parts, dim):
+    parts = jnp.moveaxis(parts, 0, dim)
+    shape = parts.shape
+    return parts.reshape(*shape[:dim], shape[dim] * shape[dim + 1], *shape[dim + 2 :])
+
+
+def doubled(value, axis):
+    size, here = (lax.axis_size(axis), lax.axis_index(axis))
+    pieces, bit = (value[None], 1)
+    while bit < size:
+        other = lax.ppermute(pieces, axis, [(i, i ^ bit) for i in range(size)])
+        low = here & bit == 0
+        pieces = jnp.concatenate([jnp.where(low, pieces, other), jnp.where(low, other, pieces)])
+        bit *= 2
+    return pieces
 
 
 def product(former, latter):
@@ -76,7 +93,7 @@
         - cross_term
         - product(cross_whole, lax.dynamic_slice_in_dim(sym_two, row_start, row_share, 1))
     )
-    lower_whole = lax.all_gather(rows_factor[0], "rows", axis=0, tiled=True)
+    lower_whole = joined_along(doubled(rows_factor[0], "rows"), 0)
     factor_cols = jnp.concatenate([cross_factor, panel_factor[0]], axis=1)
     cot_cols = jnp.concatenate([cross_next, first_cot], axis=1)
     solved_one, pending_one = panel_solve(factor_cols, cot_cols, diag_whole[0], diag_cot_whole[0])

time: 288 us -> 288 us (level)
  blocking collectives: 113 us -> 97.9 us
  waiting for transfers between devices: 68.3 us -> 79.2 us
  other arithmetic: 43.3 us -> 46.8 us
    psum x2, waiting for transfers between devices: 7.92 us -> 22.9 us  [panel_solve(): narrow = lax.psum(product(solved, factor_cols.T), 'rows')]
    all_gather x1 -> x0, blocking collectives: 15 us -> none  [on_device(): lower_whole = lax.all_gather(rows_factor[0], 'rows', axis=0, tiled=True)]
    reduce_scatter x1, waiting for transfers between devices: 13.5 us -> 0.01 us  [on_device(): lax.psum_scatter(upper_local, 'rows', scatter_dimension=0, tiled=True)]
    ppermute x0 -> x3, waiting for transfers between devices: none -> 11.7 us  [doubled(): other = lax.ppermute(pieces, axis, [(i, i ^ bit) for i in range(size)])]
    unnamed x37 -> x39, local copies, waits for them, and re-layouts: 7.06 us -> 5.46 us
  transfers between devices with their start and end apart: 5 -> 8, of which waited for: 4 -> 4; matrix products, arithmetic and copies ran while one was open for 19% -> 21% of each run, Pallas kernels for 0% -> 0%
where the time goes in v1:
time: 288 us; the launch traced here: 287 us
  blocking collectives  97.9 us (34%)
  waiting for transfers between devices  79.2 us (28%)
  other arithmetic  46.8 us (16%)
  local copies, waits for them, and re-layouts  27.9 us (10%)
  matrix products  18.9 us (7%)
  between operations  14.4 us (5%)
    another operation x9, other arithmetic, solve_upper(): lax.linalg.triangular_solve(factor, values, left_side=True, lower=True, t...  39.5 us
    reduce_scatter x1, waiting for transfers between devices, on_device(): lax.psum_scatter(lower_local, 'rows', scatter_dimension=0, tiled=True)  28.1 us
    psum x2, waiting for transfers between devices, panel_solve(): narrow = lax.psum(product(solved, factor_cols.T), 'rows')  22.9 us
    all_gather x2, blocking collectives, panel_solve(): partial_value = lax.all_gather(narrow, 'cols', axis=1, tiled=True)  18.6 us
    all_gather x2, blocking collectives, panel_solve(): cot_whole = lax.all_gather(cot_cols, 'cols', axis=0, tiled=True)  18.4 us
    unnamed x6, waiting for transfers between devices  16.6 us
    all_gather x1, blocking collectives, on_device(): lax.all_gather(diag_factor, 'rows', axis=1, tiled=True)  16.5 us
    all_gather x1, blocking collectives, on_device(): lax.all_gather(rows_factor[1], 'rows', axis=0, tiled=True)  15.3 us
  transfers between devices with their start and end apart: 8, of which 4 were waited for; matrix products, arithmetic and copies ran while one was open for 21% of the time, Pallas kernels for 0%

profile of v1, /device:TPU:0, one launch (start us, length us, event | category | flops | bytes accessed | tf_op | source)
XLA Modules:
  0.0 287.0 jit_solution(16999808795708452964)
XLA Ops:
  8.2 16.5 %all_gather.24 = f32[2,256,256]{2,0,1:T(2,128)S(1)} all-gather(f32[2,32,256]{2,0,1:T(2,128)S(1)} %copy.44), channel_id=1, replica_groups=mesh['rows'=8,'cols'=4] {'rows'}, dimensions={1}, use_global_device_ids=true | all-gather | bytes 589824 | tf_op jit(solution)/shard_map/all_gather | solution.py:70
  25.2 4.0 %while.12 = (s32[]{:T(128)}, f32[256,256]{1,0:T(8,128)S(1)}, s32[2,2]{1,0:T(2,128)S(1)}, f32[2,128,128]{2,1,0:T(8,128)S(1)}, s32[]{:T(128)}) while((s32[]{:T(128)}, f32[256,256]{1,0:T(8,128)S(1)}, s32[2,2]{1,0:T(2,128)S(1)}, f32[2,128,128]{2,1,0:T(8,128)S(1)}, s32[]{:T(128)}) %tuple.74), condition=%wide.while_cond, body=%wide.while_body.sunk | while | flops 2 | bytes 131181 | solution.py:35
  29.2 19.7 %custom-call.19 = f32[2,128,128]{1,2,0:T(8,128)S(1)} custom-call(f32[2,128,128]{2,1,0:T(8,128)S(1)} %get-tuple-element.46), custom_call_target="InvertDiagBlocksLowerTriangular" | custom-call | tf_op jit(solution)/shard_map/triangular_solve/custom-call.1 | solution.py:35
  49.7 9.0 %all-gather = f32[1,256,256]{2,1,0:T(8,128)S(1)} all-gather(f32[1,64,256]{2,1,0:T(8,128)S(1)} %slice-done), channel_id=2, replica_groups=mesh['rows'=8,'cols'=4] {'cols'}, dimensions={1}, use_global_device_ids=true | all-gather | bytes 327680 | tf_op jit(solution)/shard_map/all_gather | solution.py:46
  63.3 14.3 %all_gather.29 = f32[64,256]{0,1:T(8,128)S(1)} all-gather(f32[64,32]{0,1:T(8,128)S(1)} %copy-done.13), channel_id=1, replica_groups=mesh['rows'=8,'cols'=4] {'rows'}, dimensions={1}, use_global_device_ids=true | all-gather | bytes 73728 | tf_op jit(solution)/shard_map/all_gather | solution.py:75
  77.8 14.8 %all_gather.27 = f32[2,256,256]{2,0,1:T(2,128)S(1)} all-gather(f32[2,32,256]{2,0,1:T(2,128)S(1)} %copy.48), channel_id=1, replica_groups=mesh['rows'=8,'cols'=4] {'rows'}, dimensions={1}, use_global_device_ids=true | all-gather | bytes 589824 | tf_op jit(solution)/shard_map/all_gather | solution.py:71
  94.5 4.2 %while.11 = (s32[]{:T(128)}, f32[256,256]{0,1:T(8,128)S(1)}, s32[2,2]{1,0:T(2,128)S(1)}, f32[2,128,128]{2,1,0:T(8,128)S(1)}, s32[]{:T(128)}) while((s32[]{:T(128)}, f32[256,256]{0,1:T(8,128)S(1)}, s32[2,2]{1,0:T(2,128)S(1)}, f32[2,128,128]{2,1,0:T(8,128)S(1)}, s32[]{:T(128)}) %tuple.90), condition=%wide.while_cond.1, body=%wide.while_body.1.sunk | while | flops 2 | bytes 393321 | solution.py:35
  98.7 19.7 %custom-call.6 = f32[2,128,128]{1,2,0:T(8,128)S(1)} custom-call(f32[2,128,128]{2,1,0:T(8,128)S(1)} %get-tuple-element.21), custom_call_target="InvertDiagBlocksLowerTriangular" | custom-call | tf_op jit(solution)/shard_map/triangular_solve | solution.py:35
  118.4 9.1 %all_gather.28 = f32[256,256]{0,1:T(8,128)S(1)} all-gather(f32[256,64]{0,1:T(8,128)} %all-reduce.3.cloned.1.call-done), channel_id=1, replica_groups=mesh['rows'=8,'cols'=4] {'cols'}, dimensions={1}, use_global_device_ids=true | all-gather | bytes 327680 | tf_op jit(solution)/shard_map/all_gather | solution.py:49
  127.9 2.4 gather_fusion
  132.5 16.5 %reduce-scatter.10.cloned.1.call-done = f32[32,64]{1,0:T(8,128)} async-done(((f32[256,64]{1,0:T(8,128)}), f32[32,64]{1,0:T(8,128)}) %reduce-scatter.10.cloned.1.call-update) | async-done | bytes 8208
  150.1 9.5 %all_gather.30 = f32[256,288]{1,0:T(8,128)S(1)} all-gather(f32[64,288]{1,0:T(8,128)S(1)} %pad_maximum_fusion.10), channel_id=1, replica_groups=mesh['rows'=8,'cols'=4] {'cols'}, dimensions={0}, use_global_device_ids=true | all-gather | bytes 368640 | tf_op jit(solution)/shard_map/all_gather | solution.py:46
  162.0 1.4 fusion.32
  165.0 2.4 gather_fusion.3
  169.0 15.3 %all-gather.1 = f32[1,256,512]{2,1,0:T(8,128)S(1)} all-gather(f32[1,32,512]{2,1,0:T(8,128)S(1)} %get-tuple-element.143), channel_id=3, replica_groups=mesh['rows'=8,'cols'=4] {'rows'}, dimensions={1}, use_global_device_ids=true | all-gather | bytes 589824 | tf_op jit(solution)/shard_map/all_gather | solution.py:74
  188.4 1.5 convolution_add_fusion
  191.3 22.9 %all-reduce.5.cloned.1.call-done = f32[256,64]{0,1:T(8,128)} async-done(((f32[256,64]{0,1:T(8,128)}), f32[256,64]{0,1:T(8,128)}) %all-reduce.5.cloned.1.call-update) | async-done | bytes 65552 | tf_op jit(solution)/shard_map/psum | solution.py:48
  214.2 9.5 %all_gather.31 = f32[256,256]{0,1:T(8,128)S(1)} all-gather(f32[256,64]{0,1:T(8,128)} %all-reduce.5.cloned.1.call-done), channel_id=1, replica_groups=mesh['rows'=8,'cols'=4] {'cols'}, dimensions={1}, use_global_device_ids=true | all-gather | bytes 327680 | tf_op jit(solution)/shard_map/all_gather | solution.py:49
  224.1 2.4 gather_fusion.1
  228.7 2.4 gather_fusion.2
  232.1 1.5 collective-permute-start.2
  234.6 11.7 %collective-permute-done.2 = f32[4,32,512]{2,1,0:T(8,128)} collective-permute-done((f32[4,32,512]{2,1,0:T(8,128)S(1)}, f32[4,32,512]{2,1,0:T(8,128)}, u32[]{:S(2)}, u32[]{:S(2)}) %collective-permute-start.2) | collective-permute-done | bytes 262176 | tf_op jit(solution)/shard_map/ppermute | solution.py:19
  247.3 1.4 convolution_subtract_fusion
  250.5 28.1 %reduce-scatter.6.cloned.1.call-done = f32[32,512]{1,0:T(8,128)} async-done(((f32[256,512]{1,0:T(8,128)}), f32[32,512]{1,0:T(8,128)}) %reduce-scatter.6.cloned.1.call-update) | async-done | bytes 65552 | tf_op jit(solution)/shard_map/reduce_scatter | solution.py:106
  (147 shorter events, 40.9 us)
Async XLA Ops:
  7.2 154.8 %copy-start = (f32[256,512]{1,0:T(8,128)S(1)}, f32[256,512]{1,0:T(8,128)}, u32[]{:S(2)}) copy-start(f32[256,512]{1,0:T(8,128)} %param.12) | copy-start | bytes 1572868
  7.2 111.2 %all-reduce.3.cloned.1.call-start = ((), (), s32[]{:S(2)}) async-start(), calls=%async_computation.3 | async-start | bytes 131072 | tf_op jit(solution)/shard_map/psum | solution.py:48
  48.9 0.8 slice-start
  59.3 0.9 copy-start.7
  60.2 1.1 copy-start.4
  61.2 87.8 %reduce-scatter.10.cloned.1.call-start = ((), (), s32[]{:S(2)}) async-start(), calls=%async_computation.7 | async-start | bytes 147456
  61.3 106.1 %collective-permute-start = (f32[1,32,512]{2,1,0:T(8,128)S(1)}, f32[1,32,512]{2,1,0:T(8,128)}, u32[]{:S(2)}, u32[]{:S(2)}) collective-permute-start(f32[1,32,512]{2,1,0:T(8,128)S(1)} %slice.80), channel_id=1, source_target_pairs={{0,4},{4,0},{8,12},{12,8},{16,20},{20,16},{24,28},{28,24},{1,5},{5... | collective-permute-start | bytes 196616 | tf_op jit(solution)/shard_map/ppermute | solution.py:19
  62.6 151.6 %all-reduce.5.cloned.1.call-start = ((), (), s32[]{:S(2)}) async-start(), calls=%async_computation.5 | async-start | bytes 131072 | tf_op jit(solution)/shard_map/psum | solution.py:48
  62.6 0.7 copy-start.13
  63.3 14.4 %copy-start.14 = (f32[2,32,256]{2,1,0:T(8,128)S(1)}, f32[2,32,256]{2,1,0:T(8,128)}, u32[]{:S(2)}) copy-start(f32[2,32,256]{2,1,0:T(8,128)} %param.21) | copy-start | bytes 196612
  93.0 0.9 copy-start.8
  132.5 16.6 %copy-start.15 = (f32[64,32]{0,1:T(8,128)S(1)}, f32[64,32]{0,1:T(8,128)}, u32[]{:S(2)}) copy-start(f32[64,32]{0,1:T(8,128)} %param.19) | copy-start | bytes 24580
  161.9 86.9 %reduce-scatter.8.cloned.1.call-start = ((), (), s32[]{:S(2)}) async-start(), calls=%async_computation.6 | async-start | bytes 589824 | tf_op jit(solution)/shard_map/reduce_scatter | solution.py:87
  163.4 115.1 %reduce-scatter.6.cloned.1.call-start = ((), (), s32[]{:S(2)}) async-start(), calls=%async_computation.4 | async-start | bytes 589824 | tf_op jit(solution)/shard_map/reduce_scatter | solution.py:106
  165.0 2.5 copy-start.5
  168.3 16.0 %copy-start.3 = (f32[256,512]{1,0:T(8,128)S(1)}, f32[256,512]{1,0:T(8,128)}, u32[]{:S(2)}) copy-start(f32[256,512]{1,0:T(8,128)} %param.13) | copy-start | bytes 1572868
  169.0 62.1 %collective-permute-start.1 = (f32[2,32,512]{2,1,0:T(8,128)}, f32[2,32,512]{2,1,0:T(8,128)}, u32[]{:S(2)}, u32[]{:S(2)}) collective-permute-start(f32[2,32,512]{2,1,0:T(8,128)} %pad_maximum_fusion.7), channel_id=1, source_target_pairs={{0,8},{4,12},{8,0},{12,4},{16,24},{20,28},{24,16},{28,20},{1,9},{5... | collective-permute-start | bytes 393224 | tf_op jit(solution)/shard_map/ppermute | solution.py:19
  187.5 0.9 copy-start.6
  189.8 0.8 copy-start.9
  228.7 2.5 copy-start.2
  232.1 1.5 copy-start.10
  232.1 1.5 copy-start.11
  232.1 14.1 %collective-permute-start.2 = (f32[4,32,512]{2,1,0:T(8,128)S(1)}, f32[4,32,512]{2,1,0:T(8,128)}, u32[]{:S(2)}, u32[]{:S(2)}) collective-permute-start(f32[4,32,512]{2,1,0:T(8,128)S(1)} %pad_maximum_fusion.5), channel_id=1, source_target_pairs={{0,16},{4,20},{8,24},{12,28},{16,0},{20,4},{24,8},{28,12},{1,17},{... | collective-permute-start | bytes 786440 | tf_op jit(solution)/shard_map/ppermute | solution.py:19
  247.3 1.4 copy-start.12
  (1 other events, 0.7 us)
Sparse Core Ops, SparseCore 0:
  61.4 55.2 all-reduce.2
  119.5 29.5 reduce-scatter.9
  162.0 52.1 all-reduce.4
  216.3 30.6 reduce-scatter.7
  249.1 29.4 reduce-scatter.5
